TPU v7x, 256 devices: a whole 4x4x8 slice. The times are simulated.
256 devices in a mesh: seq: 8 (over y_hi, x), tensor: 32 (over y_lo, z, core).
Axes of the slice: x: 4, y: 4 (y_hi: 2, y_lo: 2; y = y_hi * 2 + y_lo), z: 8, core: 2. Of those that a mesh axis runs over, the one named last changes fastest.
Arguments:
- frames: bfloat16 [4096, 8192], P('seq', 'tensor'), may hold values from -6 to 6
- up_factors: bfloat16 [6, 128, 256, 256], P(None, 'tensor'), may hold values from -0.15625 to 0.15625
- down_factors: bfloat16 [6, 128, 256, 256], P(None, 'tensor'), may hold values from -0.078125 to 0.078125
- pattern: int32 [128, 5], P('tensor'), may hold values 0 or 1
- level_bits: int32 [5], replicated, may hold values from 0 to 4, each once
- taps: float32 [3, 8192], P(None, 'tensor'), may hold values from -3 to 3
- cotangent: bfloat16 [4096, 8192], P('seq', 'tensor'), may hold values from -6 to 6
Outputs:
- convolved: bfloat16 [4096, 8192], P('seq', 'tensor')
- grad_frames: bfloat16 [4096, 8192], P('seq', 'tensor')
- grad_up: float32 [6, 128, 256, 256], P(None, 'tensor', 'seq')
- grad_down: float32 [6, 128, 256, 256], P(None, 'tensor', 'seq')
Inputs may be any that keep to these rules, and one draw needn't show every extreme that they name: Level l pairs feature block i with block i xor 2^level_bits[l]; each of 0..4 appears once.
All inputs are finite; a program needn't handle non-finite values. No bound on the sum of `pattern` on one device may be relied on, other than what follows from the above.
Results may differ from a plain program's by a relative error of at most 0.012.
Values may be sent and summed in bfloat16 or wider, within the bound.
A program may use at most 64 MiB of HBM per device.

v0:
```python
import jax
import jax.numpy as jnp
from jax import lax
from jax.sharding import PartitionSpec as P

coef = 0.7978845608028654


def swapped(array, axis, stride):
    return lax.ppermute(array, axis, [(i, i ^ 1 << stride) for i in range(lax.axis_size(axis))])


def extended(array, sides, width):
    for axis, dim in sides:
        peers, length = (lax.axis_size(axis), array.shape[dim])
        up = [(i, (i + 1) % peers) for i in range(peers - 1)]
        down = [(j, i) for i, j in up]
        last = lax.slice_in_dim(array, length - width, length, axis=dim)
        leading = lax.slice_in_dim(array, 0, width, axis=dim)
        before = lax.ppermute(last, axis, up)
        after = lax.ppermute(leading, axis, down)
        array = jnp.concatenate([before, array, after], axis=dim)
    return array


def gelu_value(values):
    return 0.5 * values * (1.0 + jnp.tanh(coef * (values + 0.044715 * values * values * values)))


def gelu_slope(values):
    inner = jnp.tanh(coef * (values + 0.044715 * values * values * values))
    return 0.5 * (1.0 + inner) + 0.5 * values * (1.0 - inner * inner) * coef * (
        1.0 + 3.0 * 0.044715 * values * values
    )


def partner_rows(block_rows, bit, blocks_dev, width_block):
    rows_dev, local_width = block_rows.shape
    device_bit = bit - (blocks_dev.bit_length() - 1)
    fetched = swapped(block_rows, "tensor", device_bit)
    return fetched.reshape(rows_dev, blocks_dev, width_block)


def push_partial(partial_value, bit, blocks_dev):
    device_bit = bit - (blocks_dev.bit_length() - 1)
    return swapped(partial_value.astype(jnp.bfloat16), "tensor", device_bit).astype(
        partial_value.dtype
    )


def local(frames, up_factors, down_factors, pattern, level_bits, taps, cotangent):
    f32 = jnp.float32
    rows_dev, local_width = frames.shape
    factors, hidden_dev, width_block, _ = up_factors.shape
    levels = factors - 1
    blocks_dev = local_width // width_block
    ratio = hidden_dev // blocks_dev
    scale = 1.0 / jnp.sqrt(jnp.asarray(rows_dev * lax.axis_size("seq"), f32))
    up_four = up_factors.reshape(factors, blocks_dev, ratio, width_block, width_block)
    down_four = down_factors.reshape(factors, blocks_dev, ratio, width_block, width_block)
    level_of = [jnp.argmax(level_bits == bit) for bit in range(levels)]
    mask_of = [
        jnp.sum(jnp.where(level_bits[None, :] == bit, pattern, 0), axis=1)
        .astype(f32)
        .reshape(blocks_dev, ratio)
        for bit in range(levels)
    ]
    up_of = [
        lax.dynamic_index_in_dim(up_four, level_of[bit] + 1, 0, keepdims=False)
        for bit in range(levels)
    ]
    down_of = [
        lax.dynamic_index_in_dim(down_four, level_of[bit] + 1, 0, keepdims=False)
        for bit in range(levels)
    ]
    inputs = frames.reshape(rows_dev, blocks_dev, width_block)
    pre = jnp.einsum("rbs,bhsf->rbhf", inputs, up_four[0], preferred_element_type=f32)
    moved_inputs = []
    for bit in range(levels):
        moved = partner_rows(frames, bit, blocks_dev, width_block)
        moved_inputs.append(moved)
        pre = pre + mask_of[bit][None, :, :, None] * jnp.einsum(
            "rbs,bhsf->rbhf", moved, up_of[bit], preferred_element_type=f32
        )
    hidden = gelu_value(pre).astype(jnp.bfloat16)
    mixed = jnp.einsum("rbhf,bhfs->rbs", hidden, down_four[0], preferred_element_type=f32)
    for bit in range(levels):
        masked = hidden * mask_of[bit][None, :, :, None].astype(jnp.bfloat16)
        partial_value = jnp.einsum(
            "rbhf,bhfs->rbs", masked, down_of[bit], preferred_element_type=f32
        )
        mixed = mixed + push_partial(partial_value, bit, blocks_dev)
    mixed = mixed.reshape(rows_dev, local_width).astype(jnp.bfloat16)
    mixed_rim, cot_rim = (extended(mixed, (("seq", 0),), 1), extended(cotangent, (("seq", 0),), 1))
    mixed_f = mixed_rim.astype(f32)
    convolved = (taps[0] * mixed_f[:-2] + taps[1] * mixed_f[1:-1] + taps[2] * mixed_f[2:]).astype(
        jnp.bfloat16
    )
    cot_f = cot_rim.astype(f32)
    grad_mixed = (taps[0] * cot_f[2:] + taps[1] * cot_f[1:-1] + taps[2] * cot_f[:-2]).astype(
        jnp.bfloat16
    )
    grad_blocks = grad_mixed.reshape(rows_dev, blocks_dev, width_block)
    grad_hidden = jnp.einsum(
        "rbs,bhfs->rbhf", grad_blocks, down_four[0], preferred_element_type=f32
    )
    down_terms = [jnp.einsum("rbhf,rbs->bhfs", hidden, grad_blocks, preferred_element_type=f32)]
    for bit in range(levels):
        moved = partner_rows(grad_mixed, bit, blocks_dev, width_block)
        grad_hidden = grad_hidden + mask_of[bit][None, :, :, None] * jnp.einsum(
            "rbs,bhfs->rbhf", moved, down_of[bit], preferred_element_type=f32
        )
        down_terms.append(
            mask_of[bit][:, :, None, None]
            * jnp.einsum("rbhf,rbs->bhfs", hidden, moved, preferred_element_type=f32)
        )
    grad_pre = (grad_hidden * gelu_slope(pre)).astype(jnp.bfloat16)
    grad_in = jnp.einsum("rbhf,bhsf->rbs", grad_pre, up_four[0], preferred_element_type=f32)
    up_terms = [jnp.einsum("rbs,rbhf->bhsf", inputs, grad_pre, preferred_element_type=f32)]
    for bit in range(levels):
        masked = grad_pre * mask_of[bit][None, :, :, None].astype(jnp.bfloat16)
        partial_value = jnp.einsum("rbhf,bhsf->rbs", masked, up_of[bit], preferred_element_type=f32)
        grad_in = grad_in + push_partial(partial_value, bit, blocks_dev)
        up_terms.append(
            mask_of[bit][:, :, None, None]
            * jnp.einsum("rbs,rbhf->bhsf", moved_inputs[bit], grad_pre, preferred_element_type=f32)
        )
    grad_frames = grad_in.reshape(rows_dev, local_width).astype(jnp.bfloat16)
    term_shape = up_terms[0].shape
    shape_five = (factors,) + term_shape
    up_stack = jnp.zeros(shape_five, f32).at[0].set(up_terms[0])
    down_stack = jnp.zeros(shape_five, f32).at[0].set(down_terms[0])
    for bit in range(levels):
        up_stack = lax.dynamic_update_index_in_dim(
            up_stack, up_terms[bit + 1], level_of[bit] + 1, 0
        )
        down_stack = lax.dynamic_update_index_in_dim(
            down_stack, down_terms[bit + 1], level_of[bit] + 1, 0
        )
    up_stack = up_stack.reshape(factors, hidden_dev, term_shape[2], term_shape[3])
    down_stack = down_stack.reshape(factors, hidden_dev, term_shape[2], term_shape[3])
    grad_up, grad_down = (
        lax.psum_scatter(
            (up_stack * scale).astype(jnp.bfloat16), "seq", scatter_dimension=2, tiled=True
        ).astype(jnp.float32),
        lax.psum_scatter(
            (down_stack * scale).astype(jnp.bfloat16), "seq", scatter_dimension=2, tiled=True
        ).astype(jnp.float32),
    )
    return (convolved, grad_frames, grad_up, grad_down)


def solution(mesh):
    in_specs = (
        P("seq", "tensor"),
        P(None, "tensor", None, None),
        P(None, "tensor", None, None),
        P("tensor", None),
        P(),
        P(None, "tensor"),
        P("seq", "tensor"),
    )
    out_specs = (
        P("seq", "tensor"),
        P("seq", "tensor"),
        P(None, "tensor", "seq", None),
        P(None, "tensor", "seq", None),
    )
    return jax.shard_map(local, mesh=mesh, in_specs=in_specs, out_specs=out_specs, check_vma=False)
```

profile of v0, /device:TPU:8, one launch (start us, length us, event | category | flops | bytes accessed | tf_op | source)
XLA Modules:
  0.0 307.3 jit_solution(5022296598191540270)
XLA Ops:
  7.2 2.2 collective-permute-start.4
  9.5 5.5 %collective-permute-start.3 = (bf16[512,256]{1,0:T(8,128)(2,1)}, bf16[512,256]{1,0:T(8,128)(2,1)S(1)}, u32[]{:S(2)}, u32[]{:S(2)}) collective-permute-start(bf16[512,256]{1,0:T(8,128)(2,1)} %param.11), channel_id=1, source_target_pairs={{0,8},{1,9},{2,10},{3,11},{4,12},{5,13},{6,14},{7,15},{8,0},{9,1},... | collective-permute-start | bytes 786440 | tf_op jit(solution)/shard_map/ppermute | solution.py:10
  14.9 1.5 collective-permute-start.2
  16.4 1.0 collective-permute-start.1
  17.4 1.3 iota_reduce_fusion
  18.7 0.7 broadcast_compare_fusion.1
  19.4 1.3 iota_reduce_fusion.1
  23.3 1.3 iota_reduce_fusion.2
  25.9 1.3 iota_reduce_fusion.3
  28.5 1.3 iota_reduce_fusion.4
  31.1 0.9 select_reduce_fusion.4
  32.1 1.7 fusion.131
  33.9 1.5 fusion.119
  35.4 3.3 %collective-permute-done.2 = bf16[512,256]{1,0:T(8,128)(2,1)S(1)} collective-permute-done((bf16[512,256]{1,0:T(8,128)(2,1)}, bf16[512,256]{1,0:T(8,128)(2,1)S(1)}, u32[]{:S(2)}, u32[]{:S(2)}) %collective-permute-start.2) | collective-permute-done | bytes 262176 | tf_op jit(solution)/shard_map/ppermute | solution.py:10
  40.2 1.9 multiply_convert_fusion.2
  42.2 0.6 fusion.57
  42.8 1.7 collective-permute-start.9
  44.5 0.6 fusion.58
  45.1 2.1 collective-permute-start.8
  47.2 0.6 fusion.59
  47.8 0.6 collective-permute-start.7
  48.4 0.6 fusion.60
  49.1 1.3 collective-permute-start.6
  50.3 0.6 fusion.61
  51.3 1.3 collective-permute-start.13
  52.6 8.3 %collective-permute-done.8 = bf16[512,1,256]{2,0,1:T(8,128)(2,1)S(1)} collective-permute-done((bf16[512,1,256]{2,0,1:T(8,128)(2,1)S(1)}, bf16[512,1,256]{2,0,1:T(8,128)(2,1)S(1)}, u32[]{:S(2)}, u32[]{:S(2)}) %collective-permute-start.8) | collective-permute-done | bytes 262176 | tf_op jit(solution)/shard_map/ppermute | solution.py:10
  60.9 3.4 %collective-permute-start.12 = (bf16[1,256]{1,0:T(2,128)(2,1)S(1)}, bf16[1,256]{1,0:T(2,128)(2,1)S(1)}, u32[]{:S(2)}, u32[]{:S(2)}) collective-permute-start(bf16[1,256]{1,0:T(2,128)(2,1)S(1)} %get-tuple-element.53), channel_id=1, source_target_pairs={{0,32},{32,64},{64,96},{96,128},{128,160},{160,192},{192,224},{1,3... | collective-permute-start | bytes 1544 | tf_op jit(solution)/shard_map/ppermute | solution.py:20
  64.3 6.9 %collective-permute-done.7 = bf16[512,1,256]{2,0,1:T(8,128)(2,1)S(1)} collective-permute-done((bf16[512,1,256]{2,0,1:T(8,128)(2,1)S(1)}, bf16[512,1,256]{2,0,1:T(8,128)(2,1)S(1)}, u32[]{:S(2)}, u32[]{:S(2)}) %collective-permute-start.7) | collective-permute-done | bytes 262176 | tf_op jit(solution)/shard_map/ppermute | solution.py:10
  71.8 1.3 collective-permute-start.11
  73.1 4.5 %collective-permute-start.10 = (bf16[1,256]{1,0:T(2,128)(2,1)S(1)}, bf16[1,256]{1,0:T(2,128)(2,1)S(1)}, u32[]{:S(2)}, u32[]{:S(2)}) collective-permute-start(bf16[1,256]{1,0:T(2,128)(2,1)S(1)} %get-tuple-element.55), channel_id=1, source_target_pairs={{0,32},{32,64},{64,96},{96,128},{128,160},{160,192},{192,224},{1,3... | collective-permute-start | bytes 1544 | tf_op jit(solution)/shard_map/ppermute | solution.py:20
  77.7 1.2 collective-permute-done.10
  79.0 1.0 fusion.97
  80.0 2.7 collective-permute-start.17
  82.7 0.6 collective-permute-start.16
  83.3 2.2 collective-permute-start.15
  86.5 3.3 %scatter.9 = f32[6,4,256,256]{2,3,1,0:T(8,128)} pad(f32[1,4,256,256]{2,3,1,0:T(8,128)S(1)} %convolution_bitcast_fusion, f32[]{:T(128)} %constant.148.clone.1), padding=0_5x0_0x0_0x0_0 | pad | bytes 7340036 | tf_op jit(solution)/shard_map/scatter | solution.py:132
  90.3 5.7 %collective-permute-done.17 = bf16[512,256]{1,0:T(8,128)(2,1)S(1)} collective-permute-done((bf16[512,256]{1,0:T(8,128)(2,1)S(1)}, bf16[512,256]{1,0:T(8,128)(2,1)S(1)}, u32[]{:S(2)}, u32[]{:S(2)}) %collective-permute-start.17) | collective-permute-done | bytes 262176 | tf_op jit(solution)/shard_map/ppermute | solution.py:10
  96.4 10.4 %collective-permute-done.16 = bf16[512,256]{1,0:T(8,128)(2,1)S(1)} collective-permute-done((bf16[512,256]{1,0:T(8,128)(2,1)S(1)}, bf16[512,256]{1,0:T(8,128)(2,1)S(1)}, u32[]{:S(2)}, u32[]{:S(2)}) %collective-permute-start.16) | collective-permute-done | bytes 262176 | tf_op jit(solution)/shard_map/ppermute | solution.py:10
  108.5 2.3 fusion.6
  111.3 0.7 scatter.6
  114.2 2.5 multiply_convert_fusion.1
  116.6 6.4 %copy.109 = bf16[6,4,256,256]{3,1,0,2:T(4,128)(2,1)} copy(bf16[6,4,256,256]{2,3,1,0:T(8,128)(2,1)} %multiply_convert_fusion.1) | data formatting | bytes 6291456 | tf_op jit(solution)/shard_map/convert_element_type | solution.py:144
  123.0 1.5 fusion.41
  124.5 1.5 fusion.39
  126.0 1.5 fusion.37
  127.5 1.5 fusion.35
  129.0 1.5 fusion.33
  130.5 5.2 %multiply_convert_fusion = bf16[6,4,256,256]{2,3,1,0:T(8,128)(2,1)} fusion(f32[6,4,256,256]{2,3,1,0:T(8,128)} %fusion.33), kind=kLoop, calls=%fused_computation | loop fusion | flops 3145728 | bytes 9437184 | tf_op jit(solution)/shard_map/convert_element_type | solution.py:147
  135.7 6.3 %copy.116 = bf16[6,4,256,256]{3,1,0,2:T(4,128)(2,1)} copy(bf16[6,4,256,256]{2,3,1,0:T(8,128)(2,1)} %multiply_convert_fusion) | data formatting | bytes 6291456 | tf_op jit(solution)/shard_map/convert_element_type | solution.py:147
  142.0 1.8 fusion.52
  143.8 1.6 fusion.53
  145.4 0.6 fusion.54
  146.7 0.6 fusion.56
  147.8 3.3 %collective-permute-start.22 = (bf16[512,1,256]{2,0,1:T(8,128)(2,1)S(1)}, bf16[512,1,256]{2,0,1:T(8,128)(2,1)S(1)}, u32[]{:S(2)}, u32[]{:S(2)}) collective-permute-start(bf16[512,1,256]{2,0,1:T(8,128)(2,1)S(1)} %fusion.53), channel_id=1, source_target_pairs={{0,8},{1,9},{2,10},{3,11},{4,12},{5,13},{6,14},{7,15},{8,0},{9,1},... | collective-permute-start | bytes 786440 | tf_op jit(solution)/shard_map/ppermute | solution.py:10
  151.3 1.8 collective-permute-start.20
  154.3 1.3 collective-permute-done.23
  155.6 10.1 %collective-permute-done.22 = bf16[512,1,256]{2,0,1:T(8,128)(2,1)S(1)} collective-permute-done((bf16[512,1,256]{2,0,1:T(8,128)(2,1)S(1)}, bf16[512,1,256]{2,0,1:T(8,128)(2,1)S(1)}, u32[]{:S(2)}, u32[]{:S(2)}) %collective-permute-start.22) | collective-permute-done | bytes 262176 | tf_op jit(solution)/shard_map/ppermute | solution.py:10
  165.7 9.5 %collective-permute-done.21 = bf16[512,1,256]{2,0,1:T(8,128)(2,1)S(1)} collective-permute-done((bf16[512,1,256]{2,0,1:T(8,128)(2,1)S(1)}, bf16[512,1,256]{2,0,1:T(8,128)(2,1)S(1)}, u32[]{:S(2)}, u32[]{:S(2)}) %collective-permute-start.21) | collective-permute-done | bytes 262176 | tf_op jit(solution)/shard_map/ppermute | solution.py:10
  175.2 2.4 fusion.158
  177.6 118.4 %all-reduce.7.cloned.1.call-done = (bf16[6,4,256,256]{3,1,0,2:T(4,128)(2,1)}, bf16[6,4,256,256]{3,1,0,2:T(4,128)(2,1)}) async-done(((bf16[6,4,256,256]{3,1,0,2:T(4,128)(2,1)}, bf16[6,4,256,256]{3,1,0,2:T(4,128)(2,1)}), (bf16[6,4,256,256]{3,1,0,2:T(4,128)(2,1)}, bf16[6,4,256,256]{3,1,0,2:T(4,128)(2,1)})) %all-reduce.7.cloned.1.call-update) | async-done | bytes 6291472
  296.0 1.1 dynamic-slice_convert_fusion.1
  297.1 1.1 copy.117
  298.2 1.1 dynamic-slice_convert_fusion
  299.3 1.1 copy.118
  (84 shorter events, 10.6 us)
Async XLA Ops:
  7.2 288.8 %all-reduce.7.cloned.1.call-start = ((), (), s32[]{:S(2)}) async-start(), calls=%async_computation | async-start | bytes 12582912
  7.2 33.0 %collective-permute-start.4 = (bf16[512,256]{1,0:T(8,128)(2,1)}, bf16[512,256]{1,0:T(8,128)(2,1)S(1)}, u32[]{:S(2)}, u32[]{:S(2)}) collective-permute-start(bf16[512,256]{1,0:T(8,128)(2,1)} %param.11), channel_id=1, source_target_pairs={{0,16},{1,17},{2,18},{3,19},{4,20},{5,21},{6,22},{7,23},{8,24},{9,... | collective-permute-start | bytes 786440 | tf_op jit(solution)/shard_map/ppermute | solution.py:10
  9.5 24.4 %collective-permute-start.3 = (bf16[512,256]{1,0:T(8,128)(2,1)}, bf16[512,256]{1,0:T(8,128)(2,1)S(1)}, u32[]{:S(2)}, u32[]{:S(2)}) collective-permute-start(bf16[512,256]{1,0:T(8,128)(2,1)} %param.11), channel_id=1, source_target_pairs={{0,8},{1,9},{2,10},{3,11},{4,12},{5,13},{6,14},{7,15},{8,0},{9,1},... | collective-permute-start | bytes 786440 | tf_op jit(solution)/shard_map/ppermute | solution.py:10
  14.9 23.8 %collective-permute-start.2 = (bf16[512,256]{1,0:T(8,128)(2,1)}, bf16[512,256]{1,0:T(8,128)(2,1)S(1)}, u32[]{:S(2)}, u32[]{:S(2)}) collective-permute-start(bf16[512,256]{1,0:T(8,128)(2,1)} %param.11), channel_id=1, source_target_pairs={{0,4},{1,5},{2,6},{3,7},{4,0},{5,1},{6,2},{7,3},{8,12},{9,13},{10,... | collective-permute-start | bytes 786440 | tf_op jit(solution)/shard_map/ppermute | solution.py:10
  16.4 22.8 %collective-permute-start.1 = (bf16[512,256]{1,0:T(8,128)(2,1)}, bf16[512,256]{1,0:T(8,128)(2,1)S(1)}, u32[]{:S(2)}, u32[]{:S(2)}) collective-permute-start(bf16[512,256]{1,0:T(8,128)(2,1)} %param.11), channel_id=1, source_target_pairs={{0,2},{1,3},{2,0},{3,1},{4,6},{5,7},{6,4},{7,5},{8,10},{9,11},{10,... | collective-permute-start | bytes 786440 | tf_op jit(solution)/shard_map/ppermute | solution.py:10
  17.4 22.3 %collective-permute-start = (bf16[512,256]{1,0:T(8,128)(2,1)}, bf16[512,256]{1,0:T(8,128)(2,1)S(1)}, u32[]{:S(2)}, u32[]{:S(2)}) collective-permute-start(bf16[512,256]{1,0:T(8,128)(2,1)} %param.11), channel_id=1, source_target_pairs={{0,1},{1,0},{2,3},{3,2},{4,5},{5,4},{6,7},{7,6},{8,9},{9,8},{10,11... | collective-permute-start | bytes 786440 | tf_op jit(solution)/shard_map/ppermute | solution.py:10
  32.1 6.6 %copy-start = (bf16[6,4,256,256]{3,2,1,0:T(8,128)(2,1)S(1)}, bf16[6,4,256,256]{3,2,1,0:T(8,128)(2,1)}, u32[]{:S(2)}) copy-start(bf16[6,4,256,256]{3,2,1,0:T(8,128)(2,1)} %param.12) | copy-start | bytes 9437188
  40.2 1.9 copy-start.2
  42.8 8.5 %collective-permute-start.9 = (bf16[512,1,256]{2,0,1:T(8,128)(2,1)S(1)}, bf16[512,1,256]{2,0,1:T(8,128)(2,1)S(1)}, u32[]{:S(2)}, u32[]{:S(2)}) collective-permute-start(bf16[512,1,256]{2,0,1:T(8,128)(2,1)S(1)} %fusion.57), channel_id=1, source_target_pairs={{0,16},{1,17},{2,18},{3,19},{4,20},{5,21},{6,22},{7,23},{8,24},{9,... | collective-permute-start | bytes 786440 | tf_op jit(solution)/shard_map/ppermute | solution.py:10
  45.1 15.9 %collective-permute-start.8 = (bf16[512,1,256]{2,0,1:T(8,128)(2,1)S(1)}, bf16[512,1,256]{2,0,1:T(8,128)(2,1)S(1)}, u32[]{:S(2)}, u32[]{:S(2)}) collective-permute-start(bf16[512,1,256]{2,0,1:T(8,128)(2,1)S(1)} %fusion.58), channel_id=1, source_target_pairs={{0,8},{1,9},{2,10},{3,11},{4,12},{5,13},{6,14},{7,15},{8,0},{9,1},... | collective-permute-start | bytes 786440 | tf_op jit(solution)/shard_map/ppermute | solution.py:10
  47.8 23.4 %collective-permute-start.7 = (bf16[512,1,256]{2,0,1:T(8,128)(2,1)S(1)}, bf16[512,1,256]{2,0,1:T(8,128)(2,1)S(1)}, u32[]{:S(2)}, u32[]{:S(2)}) collective-permute-start(bf16[512,1,256]{2,0,1:T(8,128)(2,1)S(1)} %fusion.59), channel_id=1, source_target_pairs={{0,4},{1,5},{2,6},{3,7},{4,0},{5,1},{6,2},{7,3},{8,12},{9,13},{10,... | collective-permute-start | bytes 786440 | tf_op jit(solution)/shard_map/ppermute | solution.py:10
  48.4 2.8 copy-start.12
  48.4 2.8 copy-start.15
  49.1 22.1 %collective-permute-start.6 = (bf16[512,1,256]{2,0,1:T(8,128)(2,1)S(1)}, bf16[512,1,256]{2,0,1:T(8,128)(2,1)S(1)}, u32[]{:S(2)}, u32[]{:S(2)}) collective-permute-start(bf16[512,1,256]{2,0,1:T(8,128)(2,1)S(1)} %fusion.60), channel_id=1, source_target_pairs={{0,2},{1,3},{2,0},{3,1},{4,6},{5,7},{6,4},{7,5},{8,10},{9,11},{10,... | collective-permute-start | bytes 786440 | tf_op jit(solution)/shard_map/ppermute | solution.py:10
  51.0 20.2 %collective-permute-start.5 = (bf16[512,1,256]{2,0,1:T(8,128)(2,1)S(1)}, bf16[512,1,256]{2,0,1:T(8,128)(2,1)S(1)}, u32[]{:S(2)}, u32[]{:S(2)}) collective-permute-start(bf16[512,1,256]{2,0,1:T(8,128)(2,1)S(1)} %fusion.61), channel_id=1, source_target_pairs={{0,1},{1,0},{2,3},{3,2},{4,5},{5,4},{6,7},{7,6},{8,9},{9,8},{10,11... | collective-permute-start | bytes 786440 | tf_op jit(solution)/shard_map/ppermute | solution.py:10
  51.3 26.3 %collective-permute-start.13 = (bf16[1,256]{1,0:T(2,128)(2,1)S(1)}, bf16[1,256]{1,0:T(2,128)(2,1)S(1)}, u32[]{:S(2)}, u32[]{:S(2)}) collective-permute-start(bf16[1,256]{1,0:T(2,128)(2,1)S(1)} %get-tuple-element.54), channel_id=1, source_target_pairs={{32,0},{64,32},{96,64},{128,96},{160,128},{192,160},{224,192},{33,... | collective-permute-start | bytes 1544 | tf_op jit(solution)/shard_map/ppermute | solution.py:21
  60.9 16.7 %collective-permute-start.12 = (bf16[1,256]{1,0:T(2,128)(2,1)S(1)}, bf16[1,256]{1,0:T(2,128)(2,1)S(1)}, u32[]{:S(2)}, u32[]{:S(2)}) collective-permute-start(bf16[1,256]{1,0:T(2,128)(2,1)S(1)} %get-tuple-element.53), channel_id=1, source_target_pairs={{0,32},{32,64},{64,96},{96,128},{128,160},{160,192},{192,224},{1,3... | collective-permute-start | bytes 1544 | tf_op jit(solution)/shard_map/ppermute | solution.py:20
  71.8 5.9 %collective-permute-start.11 = (bf16[1,256]{1,0:T(2,128)(2,1)S(1)}, bf16[1,256]{1,0:T(2,128)(2,1)S(1)}, u32[]{:S(2)}, u32[]{:S(2)}) collective-permute-start(bf16[1,256]{1,0:T(2,128)(2,1)S(1)} %get-tuple-element.56), channel_id=1, source_target_pairs={{32,0},{64,32},{96,64},{128,96},{160,128},{192,160},{224,192},{33,... | collective-permute-start | bytes 1544 | tf_op jit(solution)/shard_map/ppermute | solution.py:21
  73.1 5.8 %collective-permute-start.10 = (bf16[1,256]{1,0:T(2,128)(2,1)S(1)}, bf16[1,256]{1,0:T(2,128)(2,1)S(1)}, u32[]{:S(2)}, u32[]{:S(2)}) collective-permute-start(bf16[1,256]{1,0:T(2,128)(2,1)S(1)} %get-tuple-element.55), channel_id=1, source_target_pairs={{0,32},{32,64},{64,96},{96,128},{128,160},{160,192},{192,224},{1,3... | collective-permute-start | bytes 1544 | tf_op jit(solution)/shard_map/ppermute | solution.py:20
  80.0 15.9 %collective-permute-start.17 = (bf16[512,256]{1,0:T(8,128)(2,1)S(1)}, bf16[512,256]{1,0:T(8,128)(2,1)S(1)}, u32[]{:S(2)}, u32[]{:S(2)}) collective-permute-start(bf16[512,256]{1,0:T(8,128)(2,1)S(1)} %get-tuple-element.60), channel_id=1, source_target_pairs={{0,8},{1,9},{2,10},{3,11},{4,12},{5,13},{6,14},{7,15},{8,0},{9,1},... | collective-permute-start | bytes 786440 | tf_op jit(solution)/shard_map/ppermute | solution.py:10
  82.7 24.1 %collective-permute-start.16 = (bf16[512,256]{1,0:T(8,128)(2,1)S(1)}, bf16[512,256]{1,0:T(8,128)(2,1)S(1)}, u32[]{:S(2)}, u32[]{:S(2)}) collective-permute-start(bf16[512,256]{1,0:T(8,128)(2,1)S(1)} %get-tuple-element.60), channel_id=1, source_target_pairs={{0,4},{1,5},{2,6},{3,7},{4,0},{5,1},{6,2},{7,3},{8,12},{9,13},{10,... | collective-permute-start | bytes 786440 | tf_op jit(solution)/shard_map/ppermute | solution.py:10
  83.3 24.0 %collective-permute-start.15 = (bf16[512,256]{1,0:T(8,128)(2,1)S(1)}, bf16[512,256]{1,0:T(8,128)(2,1)S(1)}, u32[]{:S(2)}, u32[]{:S(2)}) collective-permute-start(bf16[512,256]{1,0:T(8,128)(2,1)S(1)} %get-tuple-element.60), channel_id=1, source_target_pairs={{0,2},{1,3},{2,0},{3,1},{4,6},{5,7},{6,4},{7,5},{8,10},{9,11},{10,... | collective-permute-start | bytes 786440 | tf_op jit(solution)/shard_map/ppermute | solution.py:10
  85.5 22.3 %collective-permute-start.14 = (bf16[512,256]{1,0:T(8,128)(2,1)S(1)}, bf16[512,256]{1,0:T(8,128)(2,1)S(1)}, u32[]{:S(2)}, u32[]{:S(2)}) collective-permute-start(bf16[512,256]{1,0:T(8,128)(2,1)S(1)} %get-tuple-element.60), channel_id=1, source_target_pairs={{0,1},{1,0},{2,3},{3,2},{4,5},{5,4},{6,7},{7,6},{8,9},{9,8},{10,11... | collective-permute-start | bytes 786440 | tf_op jit(solution)/shard_map/ppermute | solution.py:10
  85.5 22.8 %collective-permute-start.18 = (bf16[512,256]{1,0:T(8,128)(2,1)S(1)}, bf16[512,256]{1,0:T(8,128)(2,1)S(1)}, u32[]{:S(2)}, u32[]{:S(2)}) collective-permute-start(bf16[512,256]{1,0:T(8,128)(2,1)S(1)} %get-tuple-element.60), channel_id=1, source_target_pairs={{0,16},{1,17},{2,18},{3,19},{4,20},{5,21},{6,22},{7,23},{8,24},{9,... | collective-permute-start | bytes 786440 | tf_op jit(solution)/shard_map/ppermute | solution.py:10
  95.9 11.4 %copy-start.3 = (bf16[512,256]{1,0:T(8,128)(2,1)}, bf16[512,256]{1,0:T(8,128)(2,1)S(1)}, u32[]{:S(2)}) copy-start(bf16[512,256]{1,0:T(8,128)(2,1)S(1)} %collective-permute-done.17) | copy-start | bytes 786436
  106.8 1.0 copy-start.5
  107.3 1.0 copy-start.7
  107.8 0.7 copy-start.9
  108.5 2.3 copy-start.13
  108.5 2.3 copy-start.11
  116.6 6.4 %copy-start.10 = (bf16[512,256]{1,0:T(8,128)(2,1)S(1)}, bf16[512,256]{1,0:T(8,128)(2,1)}, u32[]{:S(2)}) copy-start(bf16[512,256]{1,0:T(8,128)(2,1)} %copy-done.9) | copy-start | bytes 786436
  123.0 1.5 copy-start.8
  123.0 3.0 copy-start.6
  124.5 3.0 copy-start.4
  126.0 3.0 copy-start.14
  142.0 3.5 %copy-start.1 = (bf16[6,4,256,256]{3,2,1,0:T(8,128)(2,1)S(1)}, bf16[6,4,256,256]{3,2,1,0:T(8,128)(2,1)}, u32[]{:S(2)}) copy-start(bf16[6,4,256,256]{3,2,1,0:T(8,128)(2,1)} %param.12) | copy-start | bytes 9437188
  146.0 7.0 %copy-start.16 = (u32[256]{0:T(256)S(1)}, u32[256]{0:T(256)}, u32[]{:S(2)}) copy-start(u32[256]{0:T(256)} %constant.159) | copy-start | bytes 3076
  147.3 8.3 %collective-permute-start.23 = (bf16[512,1,256]{2,0,1:T(8,128)(2,1)S(1)}, bf16[512,1,256]{2,0,1:T(8,128)(2,1)S(1)}, u32[]{:S(2)}, u32[]{:S(2)}) collective-permute-start(bf16[512,1,256]{2,0,1:T(8,128)(2,1)S(1)} %fusion.52), channel_id=1, source_target_pairs={{0,16},{1,17},{2,18},{3,19},{4,20},{5,21},{6,22},{7,23},{8,24},{9,... | collective-permute-start | bytes 786440 | tf_op jit(solution)/shard_map/ppermute | solution.py:10
  147.8 17.9 %collective-permute-start.22 = (bf16[512,1,256]{2,0,1:T(8,128)(2,1)S(1)}, bf16[512,1,256]{2,0,1:T(8,128)(2,1)S(1)}, u32[]{:S(2)}, u32[]{:S(2)}) collective-permute-start(bf16[512,1,256]{2,0,1:T(8,128)(2,1)S(1)} %fusion.53), channel_id=1, source_target_pairs={{0,8},{1,9},{2,10},{3,11},{4,12},{5,13},{6,14},{7,15},{8,0},{9,1},... | collective-permute-start | bytes 786440 | tf_op jit(solution)/shard_map/ppermute | solution.py:10
  151.2 24.0 %collective-permute-start.21 = (bf16[512,1,256]{2,0,1:T(8,128)(2,1)S(1)}, bf16[512,1,256]{2,0,1:T(8,128)(2,1)S(1)}, u32[]{:S(2)}, u32[]{:S(2)}) collective-permute-start(bf16[512,1,256]{2,0,1:T(8,128)(2,1)S(1)} %fusion.54), channel_id=1, source_target_pairs={{0,4},{1,5},{2,6},{3,7},{4,0},{5,1},{6,2},{7,3},{8,12},{9,13},{10,... | collective-permute-start | bytes 786440 | tf_op jit(solution)/shard_map/ppermute | solution.py:10
  151.3 23.9 %collective-permute-start.20 = (bf16[512,1,256]{2,0,1:T(8,128)(2,1)S(1)}, bf16[512,1,256]{2,0,1:T(8,128)(2,1)S(1)}, u32[]{:S(2)}, u32[]{:S(2)}) collective-permute-start(bf16[512,1,256]{2,0,1:T(8,128)(2,1)S(1)} %fusion.55), channel_id=1, source_target_pairs={{0,2},{1,3},{2,0},{3,1},{4,6},{5,7},{6,4},{7,5},{8,10},{9,11},{10,... | collective-permute-start | bytes 786440 | tf_op jit(solution)/shard_map/ppermute | solution.py:10
  153.1 22.1 %collective-permute-start.19 = (bf16[512,1,256]{2,0,1:T(8,128)(2,1)S(1)}, bf16[512,1,256]{2,0,1:T(8,128)(2,1)}, u32[]{:S(2)}, u32[]{:S(2)}) collective-permute-start(bf16[512,1,256]{2,0,1:T(8,128)(2,1)S(1)} %fusion.56), channel_id=1, source_target_pairs={{0,1},{1,0},{2,3},{3,2},{4,5},{5,4},{6,7},{7,6},{8,9},{9,8},{10,11... | collective-permute-start | bytes 786440 | tf_op jit(solution)/shard_map/ppermute | solution.py:10
Sparse Core Ops, SparseCore 0:
  142.1 153.8 all-reduce.6
where the time goes:
time: 310 us; the launch traced here: 307 us
  waiting for transfers between devices  175 us (56%)
  starting transfers between devices  38.5 us (12%)
  matrix products  33 us (11%)
  between operations  21.7 us (7%)
  local copies, waits for them, and re-layouts  19.7 us (6%)
  other arithmetic  19.1 us (6%)
    unnamed x2, waiting for transfers between devices  118 us
    ppermute x20, waiting for transfers between devices, swapped(): lax.ppermute(array, axis, [(i, i ^ 1 << stride) for i in range(lax.axis_s...  55.5 us
    ppermute x20, starting transfers between devices, swapped(): lax.ppermute(array, axis, [(i, i ^ 1 << stride) for i in range(lax.axis_s...  27.9 us
    ppermute x2, starting transfers between devices, extended(): before = lax.ppermute(last, axis, up)  7.92 us
    dot_general x5, matrix products, local(): jnp.einsum('rbhf,rbs->bhfs', hidden, moved, preferred_element_type=f32)  7.43 us
    another operation x5, other arithmetic, local(): level_of = [jnp.argmax(level_bits == bit) for bit in range(levels)]  6.53 us
    convert_element_type x1, local copies, waits for them, and re-layouts, local(): (up_stack * scale).astype(jnp.bfloat16)  6.35 us
    convert_element_type x1, local copies, waits for them, and re-layouts, local(): (down_stack * scale).astype(jnp.bfloat16)  6.26 us
  transfers between devices with their start and end apart: 25, of which 10 were waited for; matrix products, arithmetic and copies ran while one was open for 10% of the time, Pallas kernels for 0%

commit v1 on v0

v1 whole, which is shorter than its diff:
```python
import functools

import jax
import jax.numpy as jnp
from jax import lax
from jax.experimental import pallas as pl
from jax.experimental.pallas import tpu as pltpu
from jax.sharding import PartitionSpec as P

COEF = 0.7978845608028654
F32 = jnp.float32
BF16 = jnp.bfloat16
CHUNKS = 4
N_SEMS = 160


def dot_nn(a, b):
    return jnp.dot(a, b, preferred_element_type=F32)


def dot_nt(a, b):
    return lax.dot_general(a, b, (((1,), (1,)), ((), ())), preferred_element_type=F32)


class Net:
    def __init__(self, ssem, rsem):
        self.ssem, self.rsem, self.count, self.sent = ssem, rsem, 0, []

    def send(self, src, dst, device):
        i = self.count
        self.count += 1
        copy = pltpu.make_async_remote_copy(
            src_ref=src,
            dst_ref=dst,
            send_sem=self.ssem.at[i],
            recv_sem=self.rsem.at[i],
            device_id=device,
            device_id_type=pl.DeviceIdType.MESH,
        )
        copy.start()
        self.sent.append(copy)
        return copy


def kernel(
    bits,
    pattern,
    frames,
    cot,
    taps,
    up_hbm,
    down_hbm,
    conv_out,
    gin_out,
    gup_out,
    gdown_out,
    up_raw,
    down_raw,
    wu,
    wd,
    xs,
    gs,
    xt,
    pre,
    gh,
    hid,
    hidt,
    gpre,
    part,
    part_f,
    relay,
    got,
    term,
    ra,
    rb,
    ea,
    eb,
    from_left,
    from_right,
    ysend,
    yrecv,
    mine,
    halo,
    pad,
    mix,
    wsem,
    ssem,
    rsem,
):
    rows, width = frames.shape
    chunk = rows // CHUNKS
    half = rows // 2
    ratio = wu.shape[1]
    s = lax.axis_index("seq")
    t = lax.axis_index("tensor")
    x, yh = s % 4, s // 4

    def flip(*which):
        out = t
        for b in which:
            out = out + (1 << b) * (1 - 2 * ((t // (1 << b)) % 2))
        return {"tensor": out}

    to_core, to_z1, to_z2, to_z6, to_y = flip(0), flip(1), flip(2), flip(2, 3), flip(4)
    x_right, x_left = {"seq": yh * 4 + (x + 1) % 4}, {"seq": yh * 4 + (x + 3) % 4}
    y_far = {"seq": (1 - yh) * 4 + x}
    s_next, s_prev = {"seq": (s + 1) % 8}, {"seq": (s + 7) % 8}
    net = Net(ssem, rsem)

    copy_up = pltpu.make_async_copy(up_hbm, up_raw, wsem.at[0])
    copy_down = pltpu.make_async_copy(down_hbm, down_raw, wsem.at[1])
    copy_up.start()
    copy_down.start()

    barrier = pltpu.get_barrier_semaphore()
    peers = (to_core, to_z1, to_z2, to_z6, to_y, x_right, x_left, y_far, s_next, s_prev)
    for peer in peers:
        pl.semaphore_signal(barrier, inc=1, device_id=peer, device_id_type=pl.DeviceIdType.MESH)
    pl.semaphore_wait(barrier, len(peers))

    def halo_send(ref, kind):
        return (
            net.send(ref.at[pl.ds(rows - 16, 16)], halo.at[kind, 0], s_next),
            net.send(ref.at[pl.ds(0, 16)], halo.at[kind, 1], s_prev),
        )

    def piece(c):
        return pl.ds(c * chunk, chunk)

    def spread(own, dst):
        z2 = [net.send(own.at[piece(c)], dst.at[3, piece(c)], to_z2) for c in range(CHUNKS)]
        z1 = net.send(own, dst.at[2], to_z1)
        y = net.send(own, dst.at[5], to_y)
        core = net.send(own, dst.at[1], to_core)
        return z2, z1, y, core

    def forward(z2, dst):
        z4 = []
        for c in range(CHUNKS):
            z2[c].wait_recv()
            z4.append(net.send(dst.at[3, piece(c)], dst.at[4, piece(c)], to_z6))
        return z4

    cot_halo = halo_send(cot, 0)
    x_z2, x_z1, x_y, x_core = spread(frames, xs)

    level_of = []
    for b in range(5):
        found = jnp.int32(1)
        for lev in range(1, 5):
            found = jnp.where(bits[lev] == b, lev + 1, found)
        level_of.append(found)
    mask_of = [[jnp.float32(1.0)] * ratio] + [
        [
            sum(jnp.where(bits[lev] == b, pattern[k, lev], 0) for lev in range(5)).astype(F32)
            for k in range(ratio)
        ]
        for b in range(5)
    ]

    def build(raw, out):
        for k in range(ratio):
            out[0, k] = raw[0, k]
        for b in range(5):
            for k in range(ratio):
                out[b + 1, k] = (raw[level_of[b], k].astype(F32) * mask_of[b + 1][k]).astype(BF16)

    def accumulate(acc, lhs, weights, b, dot, first=False):
        def body(k, carry):
            value = dot(lhs[...], weights[b, k])
            if first:
                acc[k] = value
            else:
                acc[k] += value
            return carry

        lax.fori_loop(0, ratio, body, 0)

    def convolve(ref, kind, before, after):
        prev = halo[kind, 0].astype(F32)[15:16]
        nxt = halo[kind, 1].astype(F32)[0:1]
        pad[pl.ds(7, 1)] = jnp.where(s > 0, prev, 0.0)
        pad[pl.ds(8, rows)] = ref[...].astype(F32)
        pad[pl.ds(8 + rows, 1)] = jnp.where(s < 7, nxt, 0.0)
        return (
            before * pad[pl.ds(7, rows)] + taps[1:2] * pad[pl.ds(8, rows)] + after * pad[pl.ds(9, rows)]
        ).astype(BF16)

    copy_up.wait()
    build(up_raw, wu)
    accumulate(pre, frames, wu, 0, dot_nn, first=True)
    for copy in cot_halo:
        copy.wait_recv()
    gs[0] = convolve(cot, 0, taps[2:3], taps[0:1])
    x_z4 = forward(x_z2, xs)
    g_z2, g_z1, g_y, g_core = spread(gs.at[0], gs)
    copy_down.wait()
    build(down_raw, wd)
    x_core.wait_recv()
    accumulate(pre, xs.at[1], wu, 1, dot_nn)
    x_y.wait_recv()
    accumulate(pre, xs.at[5], wu, 5, dot_nn)
    accumulate(pre, xs.at[3], wu, 3, dot_nn)
    x_z1.wait_recv()
    accumulate(pre, xs.at[2], wu, 2, dot_nn)
    xt[0] = frames[...].T
    for b in (1, 5, 3, 2):
        xt[b] = xs[b].T

    def partial_rows(source, weights, b, dot, at):
        total = dot(source[0, at], weights[b, 0])
        for k in range(1, ratio):
            total += dot(source[k, at], weights[b, k])
        return total

    whole = pl.ds(0, rows)

    mixed_z4 = []
    for h in range(2):
        for c in (2 * h, 2 * h + 1):
            x_z4[c].wait_recv()
        at = pl.ds(h * half, half)

        def finish(k, carry, at=at):
            u = pre[k, at] + dot_nn(xs[4, at], wu[4, k])
            square = u * u
            inner = jnp.tanh(COEF * (u + 0.044715 * square * u))
            hid[k, at] = (0.5 * u * (1.0 + inner)).astype(BF16)
            pre[k, at] = 0.5 * (1.0 + inner) + 0.5 * u * (1.0 - inner * inner) * COEF * (
                1.0 + 3.0 * 0.044715 * square
            )
            return carry

        lax.fori_loop(0, ratio, finish, 0)
        part[0, 0, at] = partial_rows(hid, wd, 4, dot_nn, at).astype(BF16)
        for c in (2 * h, 2 * h + 1):
            mixed_z4.append(net.send(part.at[0, 0, piece(c)], got.at[0, 4, piece(c)], to_z6))
    g_z4 = forward(g_z2, gs)

    def partials(phase, source, weights, dot):
        sends = []
        for slot, b, device in ((1, 2, to_z1), (2, 5, to_y), (3, 1, to_core)):
            part[phase, slot] = partial_rows(source, weights, b, dot, whole).astype(BF16)
            sends.append(net.send(part.at[phase, slot], got.at[phase, slot], device))
        part_f[phase, 0] = partial_rows(source, weights, 3, dot, whole)
        part_f[phase, 1] = partial_rows(source, weights, 0, dot, whole)
        return sends

    def combine(phase, z4):
        sends = []
        for c in range(CHUNKS):
            z4[c].wait_recv()
            at = piece(c)
            relay[phase, at] = (part_f[phase, 0, at] + got[phase, 4, at].astype(F32)).astype(BF16)
            sends.append(net.send(relay.at[phase, at], got.at[phase, 0, at], to_z2))
        return sends

    def gather_sum(phase, waits):
        for copy in waits:
            copy.wait_recv()
        total = part_f[phase, 1]
        for slot in range(4):
            total += got[phase, slot].astype(F32)
        return total.astype(BF16)

    mixed_sends = partials(0, hid, wd, dot_nn)

    for k in range(ratio):
        hidt[k] = hid[k].T

    scale = 1.0 / 64.0
    flows = {}

    def scatter_one(g):
        far, right, left = (x + 2) % 4, (x + 1) % 4, (x + 3) % 4
        flows[g] = (
            net.send(term.at[g, far], ra.at[g], x_right),
            net.send(term.at[g, 4 + far], rb.at[g], x_left),
            net.send(term.at[g, 4 + right], from_left.at[g, 1], x_right),
            net.send(term.at[g, left], from_right.at[g, 0], x_left),
        )

    def scatter_two(g):
        via_right, via_left, own_b, own_a = flows[g]
        right, left = (x + 1) % 4, (x + 3) % 4
        via_right.wait_recv()
        ea[g] = (ra[g].astype(F32) + term[g, right].astype(F32)).astype(BF16)
        sum_a = net.send(ea.at[g], from_left.at[g, 0], x_right)
        via_left.wait_recv()
        eb[g] = (rb[g].astype(F32) + term[g, 4 + left].astype(F32)).astype(BF16)
        sum_b = net.send(eb.at[g], from_right.at[g, 1], x_left)
        flows[g] = (own_b, own_a, sum_a, sum_b)

    def side_sum(g, h):
        return (
            term[g, h * 4 + x].astype(F32) + from_left[g, h].astype(F32) + from_right[g, h].astype(F32)
        )

    def scatter_three(g):
        for copy in flows[g]:
            copy.wait_recv()
        ysend[g] = side_sum(g, 1 - yh).astype(BF16)
        flows[g] = net.send(ysend.at[g], yrecv.at[g], y_far)
        mine[g] = side_sum(g, yh)

    def down_term(b):
        for k in range(ratio):
            value = dot_nn(hidt[k], gs[b]) * (mask_of[b][k] * scale)
            term[b, :, k] = value.astype(BF16).reshape(8, 32, width)
        scatter_one(b)

    def up_term(b):
        for k in range(ratio):
            value = dot_nn(xt[b], gpre[k]) * (mask_of[b][k] * scale)
            term[6 + b, :, k] = value.astype(BF16).reshape(8, 32, width)
        scatter_one(6 + b)

    down_term(0)
    accumulate(gh, gs.at[0], wd, 0, dot_nt, first=True)
    g_core.wait_recv()
    down_term(1)
    accumulate(gh, gs.at[1], wd, 1, dot_nt)
    g_y.wait_recv()
    down_term(5)
    accumulate(gh, gs.at[5], wd, 5, dot_nt)
    mixed_z2 = combine(0, mixed_z4)
    accumulate(gh, gs.at[3], wd, 3, dot_nt)
    down_term(3)
    scatter_two(0)
    g_z1.wait_recv()
    accumulate(gh, gs.at[2], wd, 2, dot_nt)
    down_term(2)
    scatter_two(1)
    xt[4] = xs[4].T

    gin_z4 = []
    for h in range(2):
        for c in (2 * h, 2 * h + 1):
            g_z4[c].wait_recv()
        at = pl.ds(h * half, half)

        def finish_grad(k, carry, at=at):
            gpre[k, at] = ((gh[k, at] + dot_nt(gs[4, at], wd[4, k])) * pre[k, at]).astype(BF16)
            return carry

        lax.fori_loop(0, ratio, finish_grad, 0)
        part[1, 0, at] = partial_rows(gpre, wu, 4, dot_nt, at).astype(BF16)
        for c in (2 * h, 2 * h + 1):
            gin_z4.append(net.send(part.at[1, 0, piece(c)], got.at[1, 4, piece(c)], to_z6))
    up_term(0)
    gin_sends = partials(1, gpre, wu, dot_nt)
    down_term(4)
    up_term(1)
    scatter_two(5)
    up_term(5)
    gin_z2 = combine(1, gin_z4)
    scatter_two(3)
    up_term(2)
    scatter_two(2)
    up_term(3)
    scatter_two(6)
    up_term(4)
    scatter_three(0)
    scatter_three(1)
    mix[...] = gather_sum(0, mixed_z2 + mixed_sends)
    mix_halo = halo_send(mix, 1)
    scatter_two(4)
    scatter_three(5)
    scatter_two(7)
    scatter_three(3)
    scatter_two(11)
    scatter_three(2)
    for copy in mix_halo:
        copy.wait_recv()
    conv_out[...] = convolve(mix, 1, taps[0:1], taps[2:3])
    scatter_two(8)
    scatter_three(6)
    scatter_three(4)
    scatter_two(9)
    scatter_three(7)
    scatter_two(10)
    scatter_three(11)
    gin_out[...] = gather_sum(1, gin_z2 + gin_sends)
    for g in (8, 9, 10):
        scatter_three(g)
    for g in range(12):
        flows[g].wait_recv()
    for base, out in ((6, gup_out), (0, gdown_out)):
        out[0] = mine[base] + yrecv[base].astype(F32)
        for lev in range(5):
            g = base + 1 + bits[lev]
            out[lev + 1] = mine[g] + yrecv[g].astype(F32)
    for copy in net.sent:
        copy.wait_send()


def local(frames, up_factors, down_factors, pattern, level_bits, taps, cotangent):
    rows, width = frames.shape
    factors, ratio, _, _ = up_factors.shape
    weights = (factors, ratio, width, width)
    tile = (ratio, 32, width)
    vmem = pl.BlockSpec(memory_space=pltpu.VMEM)
    smem = pl.BlockSpec(memory_space=pltpu.SMEM)
    anywhere = pl.BlockSpec(memory_space=pl.ANY)
    shape = jax.ShapeDtypeStruct
    return pl.pallas_call(
        kernel,
        out_shape=(
            shape((rows, width), BF16),
            shape((rows, width), BF16),
            shape((factors,) + tile, F32),
            shape((factors,) + tile, F32),
        ),
        in_specs=[smem, smem, vmem, vmem, vmem, anywhere, anywhere],
        out_specs=(vmem,) * 4,
        scratch_shapes=[
            pltpu.VMEM(weights, BF16),
            pltpu.VMEM(weights, BF16),
            pltpu.VMEM(weights, BF16),
            pltpu.VMEM(weights, BF16),
            pltpu.VMEM((6, rows, width), BF16),
            pltpu.VMEM((6, rows, width), BF16),
            pltpu.VMEM((6, width, rows), BF16),
            pltpu.VMEM((ratio, rows, width), F32),
            pltpu.VMEM((ratio, rows, width), F32),
            pltpu.VMEM((ratio, rows, width), BF16),
            pltpu.VMEM((ratio, width, rows), BF16),
            pltpu.VMEM((ratio, rows, width), BF16),
            pltpu.VMEM((2, 4, rows, width), BF16),
            pltpu.VMEM((2, 2, rows, width), F32),
            pltpu.VMEM((2, rows, width), BF16),
            pltpu.VMEM((2, 5, rows, width), BF16),
            pltpu.VMEM((12, 8) + tile, BF16),
            pltpu.VMEM((12,) + tile, BF16),
            pltpu.VMEM((12,) + tile, BF16),
            pltpu.VMEM((12,) + tile, BF16),
            pltpu.VMEM((12,) + tile, BF16),
            pltpu.VMEM((12, 2) + tile, BF16),
            pltpu.VMEM((12, 2) + tile, BF16),
            pltpu.VMEM((12,) + tile, BF16),
            pltpu.VMEM((12,) + tile, BF16),
            pltpu.VMEM((12,) + tile, F32),
            pltpu.VMEM((2, 2, 16, width), BF16),
            pltpu.VMEM((rows + 16, width), F32),
            pltpu.VMEM((rows, width), BF16),
            pltpu.SemaphoreType.DMA((2,)),
            pltpu.SemaphoreType.DMA((N_SEMS,)),
            pltpu.SemaphoreType.DMA((N_SEMS,)),
        ],
        compiler_params=pltpu.CompilerParams(
            collective_id=0, has_side_effects=True, vmem_limit_bytes=62 * 1024 * 1024
        ),
    )(level_bits, pattern, frames, cotangent, taps, up_factors, down_factors)


def solution(mesh):
    in_specs = (
        P("seq", "tensor"),
        P(None, "tensor", None, None),
        P(None, "tensor", None, None),
        P("tensor", None),
        P(),
        P(None, "tensor"),
        P("seq", "tensor"),
    )
    out_specs = (
        P("seq", "tensor"),
        P("seq", "tensor"),
        P(None, "tensor", "seq", None),
        P(None, "tensor", "seq", None),
    )
    return jax.shard_map(local, mesh=mesh, in_specs=in_specs, out_specs=out_specs, check_vma=False)
```

time: 310 us -> 114 us (0.37)
  waiting for transfers between devices: 175 us -> 0 us
  Pallas kernels: 0 us -> 106 us
  starting transfers between devices: 38.5 us -> 0 us
  matrix products: 33 us -> 0 us
  between operations: 21.7 us -> 0.65 us
  other arithmetic: 19.1 us -> 0 us
  local copies, waits for them, and re-layouts: 19.7 us -> 6.38 us
    unnamed x2 -> x0, waiting for transfers between devices: 118 us -> none
    pallas_call x0 -> x1, Pallas kernels: none -> 106 us  [local(): pl.pallas_call(kernel, out_shape=(shape((rows, width), BF16), shape((rows...]
    ppermute x24 -> x0, waiting for transfers between devices: 56.7 us -> none  [the longest x20 55.5 us: swapped(): lax.ppermute(array, axis, [(i, i ^ 1 << stride) for i in range(lax.axis_s...]
    ppermute x24 -> x0, starting transfers between devices: 38.5 us -> none  [the longest x20 27.9 us: swapped(): lax.ppermute(array, axis, [(i, i ^ 1 << stride) for i in range(lax.axis_s...]
    dot_general x36 -> x0, matrix products: 33 us -> none  [the longest x5 7.43 us: local(): jnp.einsum('rbhf,rbs->bhfs', hidden, moved, preferred_element_type=f32)]
    convert_element_type x2 -> x0, local copies, waits for them, and re-layouts: 12.6 us -> none  [the longest x1 6.35 us: local(): (up_stack * scale).astype(jnp.bfloat16)]
    convert_element_type x10 -> x0, other arithmetic: 11.1 us -> none  [the longest x1 5.21 us: local(): (down_stack * scale).astype(jnp.bfloat16)]
    another operation x5 -> x0, other arithmetic: 6.53 us -> none  [local(): level_of = [jnp.argmax(level_bits == bit) for bit in range(levels)]]
  transfers between devices with their start and end apart: 25 -> 0, of which waited for: 10 -> 0; matrix products, arithmetic and copies ran while one was open for 10% -> 0% of each run, Pallas kernels for 0% -> 0%
where the time goes in v1:
time: 114 us; the launch traced here: 113 us
  Pallas kernels  106 us (93%)
  local copies, waits for them, and re-layouts  6.38 us (6%)
    pallas_call x1, Pallas kernels, local(): pl.pallas_call(kernel, out_shape=(shape((rows, width), BF16), shape((rows...  106 us
    unnamed x6, local copies, waits for them, and re-layouts  6.38 us

profile of v1, /device:TPU:8, one launch (start us, length us, event | category | flops | bytes accessed | tf_op | source)
XLA Modules:
  0.0 113.5 jit_solution(13450141510144258336)
XLA Ops:
  0.6 106.4 %shard_map.102 = (bf16[512,256]{1,0:T(8,128)(2,1)}, bf16[512,256]{1,0:T(8,128)(2,1)}, f32[6,4,32,256]{3,2,1,0:T(8,128)}, f32[6,4,32,256]{3,2,1,0:T(8,128)}) custom-call(s32[5]{0:T(128)} %bits.1, s32[4,5]{1,0:T(4,128)} %pattern.1, bf16[512,256]{1,0:T(8,128)(2,1)} %frames.1, bf16[512,256]{1,0:T(8,128)(2,1)} %cot.1, f32[3,256]{1,0:T(4,128)} %taps.1, ...), custom_call_target="tpu_custom_call" | custom-call | tf_op jit(solution)/shard_map/pallas_call | solution.py:406
  107.1 0.0 copy-start
  107.1 1.7 %copy.15 = bf16[512,256]{1,0:T(8,128)(2,1)} copy(bf16[512,256]{1,0:T(8,128)(2,1)} %get-tuple-element.8) | data formatting | bytes 524288
  108.8 1.7 %copy.16 = bf16[512,256]{1,0:T(8,128)(2,1)} copy(bf16[512,256]{1,0:T(8,128)(2,1)} %get-tuple-element.9) | data formatting | bytes 524288
  110.5 2.1 %copy.17 = f32[6,4,32,256]{3,2,1,0:T(8,128)} copy(f32[6,4,32,256]{3,2,1,0:T(8,128)} %get-tuple-element.10) | data formatting | bytes 1572864
  112.6 0.0 copy-done
  112.6 0.9 copy.18
Async XLA Ops:
  107.1 5.5 %copy-start = (f32[6,4,32,256]{3,2,1,0:T(8,128)S(1)}, f32[6,4,32,256]{3,2,1,0:T(8,128)}, u32[]{:S(2)}) copy-start(f32[6,4,32,256]{3,2,1,0:T(8,128)} %get-tuple-element.11) | copy-start | bytes 2359300

commit v2 on v1

v2 whole, which is shorter than its diff:
```python
import functools

import jax
import jax.numpy as jnp
from jax import lax
from jax.experimental import pallas as pl
from jax.experimental.pallas import tpu as pltpu
from jax.sharding import PartitionSpec as P

COEF = 0.7978845608028654
F32 = jnp.float32
BF16 = jnp.bfloat16
CHUNKS = 4
N_SENDS = 18
N_RECVS = 66
Y_FIRST = (3, 7, 11)


def dot_nn(a, b):
    return jnp.dot(a, b, preferred_element_type=F32)


def dot_nt(a, b):
    return lax.dot_general(a, b, (((1,), (1,)), ((), ())), preferred_element_type=F32)


class Net:
    def __init__(self, ssem, rsem):
        self.ssem, self.rsem, self.n_send, self.n_recv, self.ends = ssem, rsem, 0, 0, []

    def sender(self, size):
        sem = self.ssem.at[self.n_send]
        self.n_send += 1
        self.ends.append((size, sem))
        return sem

    def receiver(self):
        sem = self.rsem.at[self.n_recv]
        self.n_recv += 1
        return sem

    def send(self, src, dst, device, ssem, rsem=None):
        rsem = self.receiver() if rsem is None else rsem
        pltpu.make_async_remote_copy(
            src_ref=src,
            dst_ref=dst,
            send_sem=ssem,
            recv_sem=rsem,
            device_id=device,
            device_id_type=pl.DeviceIdType.MESH,
        ).start()
        return dst, rsem

    def finish(self):
        for size, sem in self.ends:
            arrive((size, sem))


def arrive(flow):
    ref, sem = flow
    pltpu.make_async_copy(ref, ref, sem).wait()


def kernel(
    bits,
    pattern,
    frames_in,
    cot_in,
    taps,
    up_hbm,
    down_hbm,
    conv_hbm,
    gin_hbm,
    gup_hbm,
    gdown_hbm,
    cot,
    conv_out,
    gin_out,
    gup_out,
    gdown_out,
    up_raw,
    down_raw,
    wu,
    wd,
    xs,
    gs,
    xt,
    pre,
    gh,
    hid,
    hidt,
    gpre,
    part,
    part_f,
    relay,
    got,
    term,
    rab,
    eab,
    side,
    ybig,
    comb,
    ysend,
    yrecv_down,
    yrecv_up,
    mine,
    halo,
    pad,
    mix,
    wsem,
    ssem,
    rsem,
):
    rows, width = frames_in.shape
    frames = xs.at[0]
    yrecv = (yrecv_down, yrecv_up)
    chunk = rows // CHUNKS
    half = rows // 2
    ratio = wu.shape[1]
    s = lax.axis_index("seq")
    t = lax.axis_index("tensor")
    x, yh = s % 4, s // 4

    def flip(*which):
        out = t
        for b in which:
            out = out + (1 << b) * (1 - 2 * ((t // (1 << b)) % 2))
        return {"tensor": out}

    to_core, to_z1, to_z2, to_z6, to_y = flip(0), flip(1), flip(2), flip(2, 3), flip(4)
    x_right, x_left = {"seq": yh * 4 + (x + 1) % 4}, {"seq": yh * 4 + (x + 3) % 4}
    y_far = {"seq": (1 - yh) * 4 + x}
    s_next, s_prev = {"seq": (s + 1) % 8}, {"seq": (s + 7) % 8}
    net = Net(ssem, rsem)

    barrier = pltpu.get_barrier_semaphore()
    peers = (to_core, to_z1, to_z2, to_z6, to_y, x_right, x_left, y_far, s_next, s_prev)
    for peer in peers:
        pl.semaphore_signal(barrier, inc=1, device_id=peer, device_id_type=pl.DeviceIdType.MESH)

    def fetch(src, dst, i):
        copy = pltpu.make_async_copy(src, dst, wsem.at[i])
        copy.start()
        return copy

    copy_frames = fetch(frames_in, frames, 2)
    copy_up = fetch(up_hbm, up_raw, 0)
    copy_cot = fetch(cot_in, cot, 3)
    copy_down = fetch(down_hbm, down_raw, 1)
    pl.semaphore_wait(barrier, len(peers))

    def halo_send(ref, kind):
        out, into = net.sender(halo.at[kind]), net.receiver()
        net.send(ref.at[pl.ds(rows - 16, 16)], halo.at[kind, 0], s_next, out, into)
        net.send(ref.at[pl.ds(0, 16)], halo.at[kind, 1], s_prev, out, into)
        return halo.at[kind], into

    def piece(c):
        return pl.ds(c * chunk, chunk)

    def spread(own, dst):
        out = net.sender(dst.at[pl.ds(1, 5)])
        z2 = [net.send(own.at[piece(c)], dst.at[3, piece(c)], to_z2, out) for c in range(CHUNKS)]
        z1 = net.send(own, dst.at[2], to_z1, out)
        y = net.send(own, dst.at[5], to_y, out)
        core = net.send(own, dst.at[1], to_core, out)
        z4 = [(dst.at[4, pl.ds(h * half, half)], net.receiver()) for h in range(2)]
        return out, z2, z1, y, core, z4

    def forward(out, z2, z4, dst, c):
        arrive(z2[c])
        net.send(dst.at[3, piece(c)], dst.at[4, piece(c)], to_z6, out, z4[c // 2][1])

    cot_halo = halo_send(cot_in, 0)
    x_out, x_z2, x_z1, x_y, x_core, x_z4 = spread(frames_in, xs)

    level_of = []
    for b in range(5):
        found = jnp.int32(1)
        for lev in range(1, 5):
            found = jnp.where(bits[lev] == b, lev + 1, found)
        level_of.append(found)
    mask_of = [[jnp.float32(1.0)] * ratio] + [
        [
            sum(jnp.where(bits[lev] == b, pattern[k, lev], 0) for lev in range(5)).astype(F32)
            for k in range(ratio)
        ]
        for b in range(5)
    ]

    def build(raw, out):
        for k in range(ratio):
            out[0, k] = raw[0, k]
        for b in range(5):
            for k in range(ratio):
                out[b + 1, k] = (raw[level_of[b], k].astype(F32) * mask_of[b + 1][k]).astype(BF16)

    def accumulate(acc, lhs, weights, b, dot, first=False):
        def body(k, carry):
            value = dot(lhs[...], weights[b, k])
            if first:
                acc[k] = value
            else:
                acc[k] += value
            return carry

        lax.fori_loop(0, ratio, body, 0)

    def convolve(ref, kind, before, after):
        prev = halo[kind, 0].astype(F32)[15:16]
        nxt = halo[kind, 1].astype(F32)[0:1]
        pad[pl.ds(7, 1)] = jnp.where(s > 0, prev, 0.0)
        pad[pl.ds(8, rows)] = ref[...].astype(F32)
        pad[pl.ds(8 + rows, 1)] = jnp.where(s < 7, nxt, 0.0)
        return (
            before * pad[pl.ds(7, rows)] + taps[1:2] * pad[pl.ds(8, rows)] + after * pad[pl.ds(9, rows)]
        ).astype(BF16)

    copy_up.wait()
    build(up_raw, wu)
    copy_frames.wait()
    accumulate(pre, frames, wu, 0, dot_nn, first=True)
    forward(x_out, x_z2, x_z4, xs, 0)
    arrive(x_core)
    accumulate(pre, xs.at[1], wu, 1, dot_nn)
    forward(x_out, x_z2, x_z4, xs, 1)
    copy_down.wait()
    build(down_raw, wd)
    xt[0] = xs[0].T
    xt[1] = xs[1].T
    forward(x_out, x_z2, x_z4, xs, 2)
    arrive(x_y)
    accumulate(pre, xs.at[5], wu, 5, dot_nn)
    forward(x_out, x_z2, x_z4, xs, 3)
    copy_cot.wait()
    arrive(cot_halo)
    gs[0] = convolve(cot, 0, taps[2:3], taps[0:1])
    accumulate(pre, xs.at[3], wu, 3, dot_nn)
    arrive(x_z1)
    accumulate(pre, xs.at[2], wu, 2, dot_nn)
    for b in (5, 3, 2):
        xt[b] = xs[b].T
    for g in Y_FIRST:
        yrecv[g // 6][g % 6] = jnp.zeros(yrecv_up.shape[1:], BF16)

    def partial_rows(source, weights, b, dot, at):
        total = dot(source[0, at], weights[b, 0])
        for k in range(1, ratio):
            total += dot(source[k, at], weights[b, k])
        return total

    whole = pl.ds(0, rows)

    for h in range(2):
        arrive(x_z4[h])
        if h == 0:
            g_out, g_z2, g_z1, g_y, g_core, g_z4 = spread(gs.at[0], gs)
        at = pl.ds(h * half, half)

        def finish(k, carry, at=at):
            u = pre[k, at] + dot_nn(xs[4, at], wu[4, k])
            square = u * u
            inner = jnp.tanh(COEF * (u + 0.044715 * square * u))
            hid[k, at] = (0.5 * u * (1.0 + inner)).astype(BF16)
            pre[k, at] = 0.5 * (1.0 + inner) + 0.5 * u * (1.0 - inner * inner) * COEF * (
                1.0 + 3.0 * 0.044715 * square
            )
            return carry

        lax.fori_loop(0, ratio, finish, 0)
    for k in range(ratio):
        hidt[k] = hid[k].T

    phase_out = [net.sender(xs.at[pl.ds(1, 5)]) for _ in range(2)]
    phase_in = [(got.at[p, pl.ds(0, 4)], net.receiver()) for p in range(2)]

    def far_partial(phase, source, weights, dot):
        part[phase, 0] = partial_rows(source, weights, 4, dot, whole).astype(BF16)

    def far_send(phase):
        return [
            net.send(part.at[phase, 0, piece(c)], got.at[phase, 4, piece(c)], to_z6, phase_out[phase])
            for c in range(CHUNKS)
        ]

    def near_send(phase, slot, device):
        net.send(part.at[phase, slot], got.at[phase, slot], device, phase_out[phase], phase_in[phase][1])

    def near_partials(phase, source, weights, dot):
        for slot, b, device in ((2, 5, to_y), (3, 1, to_core), (1, 2, None)):
            part[phase, slot] = partial_rows(source, weights, b, dot, whole).astype(BF16)
            if device is not None:
                near_send(phase, slot, device)

    def kept_partials(phase, source, weights, dot):
        part_f[phase, 0] = partial_rows(source, weights, 3, dot, whole)
        part_f[phase, 1] = partial_rows(source, weights, 0, dot, whole)

    def combine(phase, z4):
        for c in range(CHUNKS):
            arrive(z4[c])
            at = piece(c)
            relay[phase, at] = (part_f[phase, 0, at] + got[phase, 4, at].astype(F32)).astype(BF16)
            net.send(
                relay.at[phase, at], got.at[phase, 0, at], to_z2, phase_out[phase], phase_in[phase][1]
            )

    def gather_sum(phase):
        arrive(phase_in[phase])
        total = part_f[phase, 1]
        for slot in range(4):
            total += got[phase, slot].astype(F32)
        return total.astype(BF16)

    scale = 1.0 / 64.0
    far, right, left = (x + 2) % 4, (x + 1) % 4, (x + 3) % 4
    group_out = {}
    flows = {}

    def halves(g):
        if g in Y_FIRST:
            i = Y_FIRST.index(g)
            first, second = pl.ds(0, ratio // 2), pl.ds(ratio // 2, ratio // 2)
            return comb, (lambda j: (i, j, first)), (lambda j: (i, j, second)), first
        return term, (lambda j: (g, j)), (lambda j: (g, 4 + j)), pl.ds(0, ratio)

    def send_across(g):
        group_out[g] = net.sender(term.at[g, pl.ds(0, 7)])
        i = Y_FIRST.index(g)
        flows[g] = net.send(term.at[g, pl.ds((1 - yh) * 4, 4)], ybig.at[i], y_far, group_out[g])

    def scatter_one(g):
        if g in Y_FIRST:
            i = Y_FIRST.index(g)
            arrive(flows[g])
            comb[i] = (term[g, pl.ds(yh * 4, 4)].astype(F32) + ybig[i].astype(F32)).astype(BF16)
        else:
            group_out[g] = net.sender(term.at[g, pl.ds(0, 7)])
        ref, a_at, b_at, ks = halves(g)
        out, via, end = group_out[g], net.receiver(), net.receiver()
        net.send(ref.at[a_at(far)], rab.at[g, 0, ks], x_right, out, via)
        net.send(ref.at[b_at(far)], rab.at[g, 1, ks], x_left, out, via)
        net.send(ref.at[b_at(right)], side.at[g, 0, 1, ks], x_right, out, end)
        net.send(ref.at[a_at(left)], side.at[g, 1, 0, ks], x_left, out, end)
        flows[g] = ((rab.at[g, :, ks], via), (side.at[g, :, :, ks], end))

    def scatter_two(g):
        ref, a_at, b_at, ks = halves(g)
        arrive(flows[g][0])
        end = flows[g][1][1]
        eab[g, 0, ks] = (rab[g, 0, ks].astype(F32) + ref[a_at(right)].astype(F32)).astype(BF16)
        net.send(eab.at[g, 0, ks], side.at[g, 0, 0, ks], x_right, group_out[g], end)
        eab[g, 1, ks] = (rab[g, 1, ks].astype(F32) + ref[b_at(left)].astype(F32)).astype(BF16)
        net.send(eab.at[g, 1, ks], side.at[g, 1, 1, ks], x_left, group_out[g], end)

    def side_sum(g, own, h, ks):
        return own.astype(F32) + side[g, 0, h, ks].astype(F32) + side[g, 1, h, ks].astype(F32)

    def scatter_three(g):
        arrive(flows[g][1])
        ref, a_at, b_at, ks = halves(g)
        if g in Y_FIRST:
            mine[g, ks] = side_sum(g, ref[a_at(x)], 0, ks)
            mine[g, pl.ds(ratio // 2, ratio // 2)] = side_sum(g, ref[b_at(x)], 1, ks)
            return
        ysend[g] = side_sum(g, term[g, (1 - yh) * 4 + x], 1 - yh, ks).astype(BF16)
        flows[g] = net.send(ysend.at[g], yrecv[g // 6].at[g % 6], y_far, group_out[g])
        mine[g] = side_sum(g, term[g, yh * 4 + x], yh, ks)

    def start(g):
        if g in Y_FIRST:
            send_across(g)
        else:
            scatter_one(g)

    def down_term(b):
        for k in range(ratio):
            value = dot_nn(hidt[k], gs[b]) * (mask_of[b][k] * scale)
            term[b, :, k] = value.astype(BF16).reshape(8, 32, width)
        start(b)

    def up_term(b):
        for k in range(ratio):
            value = dot_nn(xt[b], gpre[k]) * (mask_of[b][k] * scale)
            term[6 + b, :, k] = value.astype(BF16).reshape(8, 32, width)
        start(6 + b)

    down_term(0)
    arrive(g_core)
    down_term(1)
    accumulate(gh, gs.at[0], wd, 0, dot_nt, first=True)
    accumulate(gh, gs.at[1], wd, 1, dot_nt)
    far_partial(0, hid, wd, dot_nn)
    forward(g_out, g_z2, g_z4, gs, 0)
    arrive(g_y)
    down_term(5)
    accumulate(gh, gs.at[5], wd, 5, dot_nt)
    forward(g_out, g_z2, g_z4, gs, 1)
    scatter_two(0)
    kept_partials(0, hid, wd, dot_nn)
    forward(g_out, g_z2, g_z4, gs, 2)
    scatter_two(1)
    forward(g_out, g_z2, g_z4, gs, 3)
    down_term(3)
    near_partials(0, hid, wd, dot_nn)
    accumulate(gh, gs.at[3], wd, 3, dot_nt)
    arrive(g_z1)
    down_term(2)
    accumulate(gh, gs.at[2], wd, 2, dot_nt)
    scatter_two(5)
    xt[4] = xs[4].T
    for h in range(2):
        arrive(g_z4[h])
        at = pl.ds(h * half, half)

        def finish_grad(k, carry, at=at):
            gpre[k, at] = ((gh[k, at] + dot_nt(gs[4, at], wd[4, k])) * pre[k, at]).astype(BF16)
            return carry

        lax.fori_loop(0, ratio, finish_grad, 0)
        if h == 0:
            scatter_one(3)
    mixed_z4 = far_send(0)
    up_term(0)
    far_partial(1, gpre, wu, dot_nt)
    gin_z4 = far_send(1)
    near_send(0, 1, to_z1)
    down_term(4)
    scatter_two(2)
    up_term(1)
    up_term(2)
    up_term(5)
    scatter_two(3)
    up_term(4)
    up_term(3)
    near_partials(1, gpre, wu, dot_nt)
    kept_partials(1, gpre, wu, dot_nt)
    for g in (0, 1, 5):
        scatter_three(g)
    scatter_two(6)
    scatter_two(4)
    combine(0, mixed_z4)
    scatter_two(8)
    scatter_one(7)
    scatter_two(10)
    combine(1, gin_z4)
    near_send(1, 1, to_z1)
    for g in (2, 3):
        scatter_three(g)
    scatter_one(11)
    scatter_two(9)
    scatter_three(6)
    scatter_three(4)
    scatter_two(7)
    mix[...] = gather_sum(0)
    mix_halo = halo_send(mix, 1)
    scatter_two(11)
    scatter_three(8)
    scatter_three(10)
    scatter_three(9)

    def final(base, out):
        there = yrecv[base // 6]
        out[0] = mine[base] + there[0].astype(F32)
        for lev in range(5):
            b = 1 + bits[lev]
            out[lev + 1] = mine[base + b] + there[b].astype(F32)

    for g in (0, 1, 5, 2, 4):
        arrive(flows[g])
    final(0, gdown_out)
    put_gdown = fetch(gdown_out, gdown_hbm, 4)
    arrive(mix_halo)
    conv_out[...] = convolve(mix, 1, taps[0:1], taps[2:3])
    put_conv = fetch(conv_out, conv_hbm, 5)
    scatter_three(7)
    scatter_three(11)
    gin_out[...] = gather_sum(1)
    put_gin = fetch(gin_out, gin_hbm, 6)
    for g in (6, 8, 10, 9):
        arrive(flows[g])
    final(6, gup_out)
    put_gup = fetch(gup_out, gup_hbm, 7)
    net.finish()
    for copy in (put_gdown, put_conv, put_gin, put_gup):
        copy.wait()


def write_kernel(*refs):
    ins, outs, held, sems = refs[:4], refs[4:8], refs[8:12], refs[12]
    loads = [pltpu.make_async_copy(ins[i], held[i], sems.at[i]) for i in range(4)]
    stores = [pltpu.make_async_copy(held[i], outs[i], sems.at[4 + i]) for i in range(4)]
    for load in loads:
        load.start()
    for load, store in zip(loads, stores):
        load.wait()
        store.start()
    for store in stores:
        store.wait()


def local(frames, up_factors, down_factors, pattern, level_bits, taps, cotangent):
    rows, width = frames.shape
    factors, ratio, _, _ = up_factors.shape
    weights = (factors, ratio, width, width)
    tile = (ratio, 32, width)
    vmem = pl.BlockSpec(memory_space=pltpu.VMEM)
    smem = pl.BlockSpec(memory_space=pltpu.SMEM)
    anywhere = pl.BlockSpec(memory_space=pl.ANY)
    shape = jax.ShapeDtypeStruct
    results = (
        shape((rows, width), BF16),
        shape((rows, width), BF16),
        shape((factors,) + tile, F32),
        shape((factors,) + tile, F32),
    )
    held = [pltpu.VMEM(each.shape, each.dtype) for each in results]
    computed = pl.pallas_call(
        kernel,
        out_shape=results,
        in_specs=[smem, smem, anywhere, anywhere, vmem, anywhere, anywhere],
        out_specs=(anywhere,) * 4,
        scratch_shapes=[
            pltpu.VMEM((rows, width), BF16),
            *held,
            pltpu.VMEM(weights, BF16),
            pltpu.VMEM(weights, BF16),
            pltpu.VMEM(weights, BF16),
            pltpu.VMEM(weights, BF16),
            pltpu.VMEM((6, rows, width), BF16),
            pltpu.VMEM((6, rows, width), BF16),
            pltpu.VMEM((6, width, rows), BF16),
            pltpu.VMEM((ratio, rows, width), F32),
            pltpu.VMEM((ratio, rows, width), F32),
            pltpu.VMEM((ratio, rows, width), BF16),
            pltpu.VMEM((ratio, width, rows), BF16),
            pltpu.VMEM((ratio, rows, width), BF16),
            pltpu.VMEM((2, 4, rows, width), BF16),
            pltpu.VMEM((2, 2, rows, width), F32),
            pltpu.VMEM((2, rows, width), BF16),
            pltpu.VMEM((2, 5, rows, width), BF16),
            pltpu.VMEM((12, 8) + tile, BF16),
            pltpu.VMEM((12, 2) + tile, BF16),
            pltpu.VMEM((12, 2) + tile, BF16),
            pltpu.VMEM((12, 2, 2) + tile, BF16),
            pltpu.VMEM((len(Y_FIRST), 4) + tile, BF16),
            pltpu.VMEM((len(Y_FIRST), 4) + tile, BF16),
            pltpu.VMEM((12,) + tile, BF16),
            pltpu.VMEM((6,) + tile, BF16),
            pltpu.VMEM((6,) + tile, BF16),
            pltpu.VMEM((12,) + tile, F32),
            pltpu.VMEM((2, 2, 16, width), BF16),
            pltpu.VMEM((rows + 16, width), F32),
            pltpu.VMEM((rows, width), BF16),
            pltpu.SemaphoreType.DMA((8,)),
            pltpu.SemaphoreType.DMA((N_SENDS,)),
            pltpu.SemaphoreType.DMA((N_RECVS,)),
        ],
        compiler_params=pltpu.CompilerParams(
            collective_id=0, has_side_effects=True, vmem_limit_bytes=62 * 1024 * 1024
        ),
    )(level_bits, pattern, frames, cotangent, taps, up_factors, down_factors)
    return pl.pallas_call(
        write_kernel,
        out_shape=results,
        in_specs=[anywhere] * 4,
        out_specs=(anywhere,) * 4,
        scratch_shapes=[*held, pltpu.SemaphoreType.DMA((8,))],
    )(*computed)


def solution(mesh):
    in_specs = (
        P("seq", "tensor"),
        P(None, "tensor", None, None),
        P(None, "tensor", None, None),
        P("tensor", None),
        P(),
        P(None, "tensor"),
        P("seq", "tensor"),
    )
    out_specs = (
        P("seq", "tensor"),
        P("seq", "tensor"),
        P(None, "tensor", "seq", None),
        P(None, "tensor", "seq", None),
    )
    return jax.shard_map(local, mesh=mesh, in_specs=in_specs, out_specs=out_specs, check_vma=False)
```

time: 114 us -> 93.3 us (0.82)
  Pallas kernels: 106 us -> 92.4 us
  local copies, waits for them, and re-layouts: 6.38 us -> 0 us
    pallas_call x1 -> x2, Pallas kernels: 106 us -> 92.4 us  [the longest x1 89.9 us: local(): pl.pallas_call(kernel, out_shape=results, in_specs=[smem, smem, anywhere,...]
    unnamed x6 -> x0, local copies, waits for them, and re-layouts: 6.38 us -> none
where the time goes in v2:
time: 93.3 us; the launch traced here: 93.2 us
  Pallas kernels  92.4 us (99%)
    pallas_call x1, Pallas kernels, local(): pl.pallas_call(kernel, out_shape=results, in_specs=[smem, smem, anywhere,...  89.9 us
    pallas_call x1, Pallas kernels, local(): pl.pallas_call(write_kernel, out_shape=results, in_specs=[anywhere] * 4,...  2.51 us

profile of v2, /device:TPU:8, one launch (start us, length us, event | category | flops | bytes accessed | tf_op | source)
XLA Modules:
  0.0 93.2 jit_solution(14374816981184672659)
XLA Ops:
  0.6 89.9 %shard_map.102 = (bf16[512,256]{1,0:T(8,128)(2,1)}, bf16[512,256]{1,0:T(8,128)(2,1)}, f32[6,4,32,256]{3,2,1,0:T(8,128)}, f32[6,4,32,256]{3,2,1,0:T(8,128)}) custom-call(s32[5]{0:T(128)} %bits.1, s32[4,5]{1,0:T(4,128)} %pattern.1, bf16[512,256]{1,0:T(8,128)(2,1)} %frames_in.1, bf16[512,256]{1,0:T(8,128)(2,1)} %cot_in.1, f32[3,256]{1,0:T(4,128)} %taps.1, ...), custom_call_target="tpu_custom_call" | custom-call | tf_op jit(solution)/shard_map/pallas_call | solution.py:518
  90.5 2.5 %shard_map.103 = (bf16[512,256]{1,0:T(8,128)(2,1)}, bf16[512,256]{1,0:T(8,128)(2,1)}, f32[6,4,32,256]{3,2,1,0:T(8,128)}, f32[6,4,32,256]{3,2,1,0:T(8,128)}) custom-call(bf16[512,256]{1,0:T(8,128)(2,1)} %get-tuple-element.8.refs_0_, bf16[512,256]{1,0:T(8,128)(2,1)} %get-tuple-element.9.refs_1_, f32[6,4,32,256]{3,2,1,0:T(8,128)} %get-tuple-element.10.refs_2_, ...), custom_call_target="tpu_custom_call" | custom-call | tf_op jit(solution)/shard_map/pallas_call | solution.py:563

commit v3 on v2

--- a/solution.py
+++ b/solution.py
@@ -11,8 +11,9 @@
 F32 = jnp.float32
 BF16 = jnp.bfloat16
 CHUNKS = 4
+PIECES = 16
 N_SENDS = 18
-N_RECVS = 66
+N_RECVS = 90
 Y_FIRST = (3, 7, 11)
 
 
@@ -69,15 +70,11 @@
     taps,
     up_hbm,
     down_hbm,
-    conv_hbm,
-    gin_hbm,
-    gup_hbm,
-    gdown_hbm,
-    cot,
     conv_out,
     gin_out,
     gup_out,
     gdown_out,
+    cot,
     up_raw,
     down_raw,
     wu,
@@ -107,6 +104,7 @@
     halo,
     pad,
     mix,
+    meet,
     wsem,
     ssem,
     rsem,
@@ -155,21 +153,35 @@
         net.send(ref.at[pl.ds(0, 16)], halo.at[kind, 1], s_prev, out, into)
         return halo.at[kind], into
 
+    def ready(i, others):
+        for other in others:
+            pl.semaphore_signal(
+                meet.at[i], inc=1, device_id=other, device_id_type=pl.DeviceIdType.MESH
+            )
+
+    def await_ready(i, others):
+        pl.semaphore_wait(meet.at[i], len(others))
+
     def piece(c):
         return pl.ds(c * chunk, chunk)
 
+    def small(c):
+        return pl.ds(c * (rows // PIECES), rows // PIECES)
+
     def spread(own, dst):
         out = net.sender(dst.at[pl.ds(1, 5)])
-        z2 = [net.send(own.at[piece(c)], dst.at[3, piece(c)], to_z2, out) for c in range(CHUNKS)]
+        z2 = [net.send(own.at[small(c)], dst.at[3, small(c)], to_z2, out) for c in range(PIECES)]
         z1 = net.send(own, dst.at[2], to_z1, out)
         y = net.send(own, dst.at[5], to_y, out)
         core = net.send(own, dst.at[1], to_core, out)
         z4 = [(dst.at[4, pl.ds(h * half, half)], net.receiver()) for h in range(2)]
         return out, z2, z1, y, core, z4
 
-    def forward(out, z2, z4, dst, c):
-        arrive(z2[c])
-        net.send(dst.at[3, piece(c)], dst.at[4, piece(c)], to_z6, out, z4[c // 2][1])
+    def forward(out, z2, z4, dst, part):
+        each = PIECES // 4
+        for c in range(part * each, (part + 1) * each):
+            arrive(z2[c])
+            net.send(dst.at[3, small(c)], dst.at[4, small(c)], to_z6, out, z4[2 * c // PIECES][1])
 
     cot_halo = halo_send(cot_in, 0)
     x_out, x_z2, x_z1, x_y, x_core, x_z4 = spread(frames_in, xs)
@@ -411,6 +423,12 @@
     xt[4] = xs[4].T
     for h in range(2):
         arrive(g_z4[h])
+        if h == 0:
+            ready(0, (to_core, to_z1))
+            await_ready(0, (to_core, to_z1))
+            mixed_z4 = far_send(0)
+        else:
+            near_send(0, 1, to_z1)
         at = pl.ds(h * half, half)
 
         def finish_grad(k, carry, at=at):
@@ -420,11 +438,9 @@
         lax.fori_loop(0, ratio, finish_grad, 0)
         if h == 0:
             scatter_one(3)
-    mixed_z4 = far_send(0)
     up_term(0)
     far_partial(1, gpre, wu, dot_nt)
     gin_z4 = far_send(1)
-    near_send(0, 1, to_z1)
     down_term(4)
     scatter_two(2)
     up_term(1)
@@ -469,31 +485,21 @@
     for g in (0, 1, 5, 2, 4):
         arrive(flows[g])
     final(0, gdown_out)
-    put_gdown = fetch(gdown_out, gdown_hbm, 4)
     arrive(mix_halo)
     conv_out[...] = convolve(mix, 1, taps[0:1], taps[2:3])
-    put_conv = fetch(conv_out, conv_hbm, 5)
     scatter_three(7)
     scatter_three(11)
     gin_out[...] = gather_sum(1)
-    put_gin = fetch(gin_out, gin_hbm, 6)
     for g in (6, 8, 10, 9):
         arrive(flows[g])
     final(6, gup_out)
-    put_gup = fetch(gup_out, gup_hbm, 7)
     net.finish()
-    for copy in (put_gdown, put_conv, put_gin, put_gup):
-        copy.wait()
 
 
 def write_kernel(*refs):
-    ins, outs, held, sems = refs[:4], refs[4:8], refs[8:12], refs[12]
-    loads = [pltpu.make_async_copy(ins[i], held[i], sems.at[i]) for i in range(4)]
-    stores = [pltpu.make_async_copy(held[i], outs[i], sems.at[4 + i]) for i in range(4)]
-    for load in loads:
-        load.start()
-    for load, store in zip(loads, stores):
-        load.wait()
+    ins, outs, sems = refs[:4], refs[4:8], refs[8]
+    stores = [pltpu.make_async_copy(ins[i], outs[i], sems.at[i]) for i in range(4)]
+    for store in stores:
         store.start()
     for store in stores:
         store.wait()
@@ -514,15 +520,14 @@
         shape((factors,) + tile, F32),
         shape((factors,) + tile, F32),
     )
-    held = [pltpu.VMEM(each.shape, each.dtype) for each in results]
+    held = tuple(pltpu.VMEM(each.shape, each.dtype) for each in results)
     computed = pl.pallas_call(
         kernel,
-        out_shape=results,
+        out_shape=held,
         in_specs=[smem, smem, anywhere, anywhere, vmem, anywhere, anywhere],
-        out_specs=(anywhere,) * 4,
+        out_specs=(vmem,) * 4,
         scratch_shapes=[
             pltpu.VMEM((rows, width), BF16),
-            *held,
             pltpu.VMEM(weights, BF16),
             pltpu.VMEM(weights, BF16),
             pltpu.VMEM(weights, BF16),
@@ -552,20 +557,22 @@
             pltpu.VMEM((2, 2, 16, width), BF16),
             pltpu.VMEM((rows + 16, width), F32),
             pltpu.VMEM((rows, width), BF16),
+            pltpu.SemaphoreType.REGULAR((3,)),
             pltpu.SemaphoreType.DMA((8,)),
             pltpu.SemaphoreType.DMA((N_SENDS,)),
             pltpu.SemaphoreType.DMA((N_RECVS,)),
         ],
         compiler_params=pltpu.CompilerParams(
-            collective_id=0, has_side_effects=True, vmem_limit_bytes=62 * 1024 * 1024
+            collective_id=0, has_side_effects=True, vmem_limit_bytes=56 * 1024 * 1024
         ),
     )(level_bits, pattern, frames, cotangent, taps, up_factors, down_factors)
     return pl.pallas_call(
         write_kernel,
         out_shape=results,
-        in_specs=[anywhere] * 4,
+        in_specs=[vmem] * 4,
         out_specs=(anywhere,) * 4,
-        scratch_shapes=[*held, pltpu.SemaphoreType.DMA((8,))],
+        scratch_shapes=[pltpu.SemaphoreType.DMA((4,))],
+        compiler_params=pltpu.CompilerParams(vmem_limit_bytes=4 * 1024 * 1024),
     )(*computed)
 
 

time: 93.3 us -> 90.7 us (0.972)
  Pallas kernels: 92.4 us -> 89.2 us
    pallas_call x2, Pallas kernels: 92.4 us -> 89.2 us  [the longest x1 87.9 us: local(): pl.pallas_call(kernel, out_shape=held, in_specs=[smem, smem, anywhere, an...]
where the time goes in v3:
time: 90.7 us; the launch traced here: 90 us
  Pallas kernels  89.2 us (98%)
    pallas_call x1, Pallas kernels, local(): pl.pallas_call(kernel, out_shape=held, in_specs=[smem, smem, anywhere, an...  87.9 us

profile of v3, /device:TPU:8, one launch (start us, length us, event | category | flops | bytes accessed | tf_op | source)
XLA Modules:
  0.0 90.0 jit_solution(12588869946806596100)
XLA Ops:
  0.6 87.9 %shard_map.102 = (bf16[512,256]{1,0:T(8,128)(2,1)S(1)}, bf16[512,256]{1,0:T(8,128)(2,1)S(1)}, f32[6,4,32,256]{3,2,1,0:T(8,128)S(1)}, f32[6,4,32,256]{3,2,1,0:T(8,128)S(1)}) custom-call(s32[5]{0:T(128)} %bits.1, s32[4,5]{1,0:T(4,128)} %pattern.1, bf16[512,256]{1,0:T(8,128)(2,1)} %frames_in.1, bf16[512,256]{1,0:T(8,128)(2,1)} %cot_in.1, f32[3,256]{1,0:T(4,128)} %taps.1, ...), custom_call_target="tpu_custom_call" | custom-call | tf_op jit(solution)/shard_map/pallas_call | solution.py:524
  88.5 1.3 %shard_map.103 = (bf16[512,256]{1,0:T(8,128)(2,1)}, bf16[512,256]{1,0:T(8,128)(2,1)}, f32[6,4,32,256]{3,2,1,0:T(8,128)}, f32[6,4,32,256]{3,2,1,0:T(8,128)}) custom-call(bf16[512,256]{1,0:T(8,128)(2,1)S(1)} %get-tuple-element.8.refs_0_, bf16[512,256]{1,0:T(8,128)(2,1)S(1)} %get-tuple-element.9.refs_1_, f32[6,4,32,256]{3,2,1,0:T(8,128)S(1)} %get-tuple-element.10.refs_2_, ...), custom_call_target="tpu_custom_call" | custom-call | tf_op jit(solution)/shard_map/pallas_call | solution.py:569

commit v4 on v3

--- a/solution.py
+++ b/solution.py
@@ -263,10 +263,9 @@
 
     whole = pl.ds(0, rows)
 
+    g_out, g_z2, g_z1, g_y, g_core, g_z4 = spread(gs.at[0], gs)
     for h in range(2):
         arrive(x_z4[h])
-        if h == 0:
-            g_out, g_z2, g_z1, g_y, g_core, g_z4 = spread(gs.at[0], gs)
         at = pl.ds(h * half, half)
 
         def finish(k, carry, at=at):

time: 90.7 us -> 90 us (level); the launches traced: 90 us -> 88.2 us
  Pallas kernels: 89.2 us -> 87.4 us
    pallas_call x1, Pallas kernels: 87.9 us -> 86.1 us  [local(): pl.pallas_call(kernel, out_shape=held, in_specs=[smem, smem, anywhere, an...]
where the time goes in v4:
time: 90 us; the launch traced here: 88.2 us
  Pallas kernels  87.4 us (97%)
    pallas_call x1, Pallas kernels, local(): pl.pallas_call(kernel, out_shape=held, in_specs=[smem, smem, anywhere, an...  86.1 us

profile of v4, /device:TPU:8, one launch (start us, length us, event | category | flops | bytes accessed | tf_op | source)
XLA Modules:
  0.0 88.2 jit_solution(8146759612632518020)
XLA Ops:
  0.6 86.1 %shard_map.102 = (bf16[512,256]{1,0:T(8,128)(2,1)S(1)}, bf16[512,256]{1,0:T(8,128)(2,1)S(1)}, f32[6,4,32,256]{3,2,1,0:T(8,128)S(1)}, f32[6,4,32,256]{3,2,1,0:T(8,128)S(1)}) custom-call(s32[5]{0:T(128)} %bits.1, s32[4,5]{1,0:T(4,128)} %pattern.1, bf16[512,256]{1,0:T(8,128)(2,1)} %frames_in.1, bf16[512,256]{1,0:T(8,128)(2,1)} %cot_in.1, f32[3,256]{1,0:T(4,128)} %taps.1, ...), custom_call_target="tpu_custom_call" | custom-call | tf_op jit(solution)/shard_map/pallas_call | solution.py:523
  86.7 1.3 %shard_map.103 = (bf16[512,256]{1,0:T(8,128)(2,1)}, bf16[512,256]{1,0:T(8,128)(2,1)}, f32[6,4,32,256]{3,2,1,0:T(8,128)}, f32[6,4,32,256]{3,2,1,0:T(8,128)}) custom-call(bf16[512,256]{1,0:T(8,128)(2,1)S(1)} %get-tuple-element.8.refs_0_, bf16[512,256]{1,0:T(8,128)(2,1)S(1)} %get-tuple-element.9.refs_1_, f32[6,4,32,256]{3,2,1,0:T(8,128)S(1)} %get-tuple-element.10.refs_2_, ...), custom_call_target="tpu_custom_call" | custom-call | tf_op jit(solution)/shard_map/pallas_call | solution.py:568
